TPU v7x, 32 devices: a whole 2x2x4 slice. The times are simulated.
32 devices in a mesh: groups: 2 (over x), frame: 16 (over z, y, core).
Axes of the slice: x: 2, y: 2, z: 4, core: 2. Of those that a mesh axis runs over, the one named last changes fastest.
Arguments:
- lowres: bfloat16 [32, 64, 128], P(('groups', 'frame')), parts along dimension 0, may hold values from -6 to 6
- noisy: bfloat16 [32, 8, 64, 128], P(('groups', 'frame')), parts along dimension 0, may hold values from -6 to 6
- starts: int32 [8], P('groups'), parts along dimension 0, may hold values from 0 to 8, as said below
- blend: int32 [8, 8], P('groups'), parts along dimension 0, may hold values from 1 to 4
- assign: int32 [32], P('groups'), parts along dimension 0, may hold values from 0 to 15, each once
- base_w: bfloat16 [3, 128, 128], replicated, may hold values from -0.3125 to 0.3125
- cond_w: bfloat16 [128, 128], replicated, may hold values from -0.5 to 0.5
- noise_w: bfloat16 [128, 128], replicated, may hold values from -0.5 to 0.5
- gains: float32 [3, 128], replicated, may hold values from 0.25 to 1.75
- tconv: float32 [3, 3, 128], replicated, may hold values from -3 to 3
- mlp_in: bfloat16 [3, 128, 512], replicated, may hold values from -0.5 to 0.5
- mlp_out: bfloat16 [3, 512, 128], replicated, may hold values from -0.25 to 0.25
Outputs:
- video: bfloat16 [32, 256, 128], P(('groups', 'frame')), parts along dimension 0
There are 2 independent parts, one for each index of `groups`. A program takes and returns all parts, laid end to end along the dimension named above; an argument that names none is the same for every part. Nothing has to cross between parts.
Inputs may be any that keep to these rules, and one draw needn't show every extreme that they name: Window k covers frames starts[k] to starts[k] + 7; every frame lies in some window; the first window starts at 0 and the last at 8.
All inputs are finite; a program needn't handle non-finite values.
Results may differ from a plain program's by a relative error of at most 0.0059.
Values may be sent and summed in bfloat16 or wider, within the bound.
No kernel may reach another device: no remote copies, remote signals or barrier semaphores. Data moves between devices by JAX's collectives and lax.ppermute only.
A program may use at most 64 MiB of HBM per device.

v0:
```python
import jax
import jax.numpy as jnp
from jax import lax
from jax.sharding import PartitionSpec as P

TILES = 4


def padded_2(cells, sides, width):
    for axis, dim in sides:
        count = lax.axis_size(axis)
        ends = count - 1
        head = lax.slice_in_dim(cells, 0, width, axis=dim)
        tail = lax.slice_in_dim(cells, cells.shape[dim] - width, cells.shape[dim], axis=dim)
        cells = jnp.concatenate(
            [
                lax.ppermute(tail, axis, [(i, (i + 1) % count) for i in range(ends)]),
                cells,
                lax.ppermute(head, axis, [((i + 1) % count, i) for i in range(ends)]),
            ],
            axis=dim,
        )
    return cells


def refine_block(cond, noisy_item, cond_w, noise_w, gains, tconv, mlp_in, mlp_out):
    frame_count, positions, channels = cond.shape
    row_count = frame_count * positions
    state = jnp.dot(cond.reshape(row_count, channels), cond_w, preferred_element_type=jnp.float32)
    state = state + jnp.dot(
        noisy_item.reshape(row_count, channels), noise_w, preferred_element_type=jnp.float32
    )
    for layer_id in range(gains.shape[0]):
        inverse = lax.rsqrt(jnp.mean(state * state, axis=-1, keepdims=True) + 1e-06)
        normed = (state * inverse * gains[layer_id]).reshape(frame_count, positions, channels)
        zeros_frame = jnp.zeros_like(normed[:1])
        before = jnp.concatenate([zeros_frame, normed[:-1]], 0)
        behind = jnp.concatenate([normed[1:], zeros_frame], 0)
        mixed_rows = (
            normed
            + tconv[layer_id, 0] * before
            + tconv[layer_id, 1] * normed
            + tconv[layer_id, 2] * behind
        )
        mixed_rows = mixed_rows.reshape(row_count, channels).astype(jnp.bfloat16)
        hidden = jax.nn.silu(
            jnp.dot(mixed_rows, mlp_in[layer_id], preferred_element_type=jnp.float32)
        ).astype(jnp.bfloat16)
        state = state + jnp.dot(hidden, mlp_out[layer_id], preferred_element_type=jnp.float32)
    return state.astype(jnp.bfloat16).reshape(frame_count, positions, channels)


def refine(cond, noisy_item, cond_w, noise_w, gains, tconv, mlp_in, mlp_out):
    frame_count, positions, channels = cond.shape
    block_count = positions // positions
    cond_blocks = jnp.transpose(
        cond.reshape(frame_count, block_count, positions, channels), (1, 0, 2, 3)
    )
    noisy_blocks = jnp.transpose(
        noisy_item.reshape(frame_count, block_count, positions, channels), (1, 0, 2, 3)
    )

    def one_block(pair):
        return refine_block(pair[0], pair[1], cond_w, noise_w, gains, tconv, mlp_in, mlp_out)

    outputs = lax.map(one_block, (cond_blocks, noisy_blocks))
    return jnp.transpose(outputs, (1, 0, 2, 3)).reshape(frame_count, positions, channels)


def on_device(
    lowres, noisy, starts, blend, assign, base_w, cond_w, noise_w, gains, tconv, mlp_in, mlp_out
):
    frame_total = assign.shape[0]
    window_len = noisy.shape[1]
    tile_pos = noisy.shape[2]
    channels = noisy.shape[3]
    low_pos = lowres.shape[1] // TILES
    padded = padded_2(lowres, (("frame", 0),), 1)
    total = jnp.dot(padded[0], base_w[0], preferred_element_type=jnp.float32)
    total = total + jnp.dot(padded[1], base_w[1], preferred_element_type=jnp.float32)
    total = total + jnp.dot(padded[2], base_w[2], preferred_element_type=jnp.float32)
    base_frame = (lowres[0].astype(jnp.float32) + jax.nn.silu(total)).astype(jnp.bfloat16)
    own_index = lax.axis_index("frame")
    item_id = assign[own_index]
    own_start = starts[item_id // TILES]
    tile_rows = base_frame.reshape(TILES, low_pos * channels)
    picker = (assign[:, None] % TILES == jnp.arange(TILES, dtype=jnp.int32)[None, :]).astype(
        jnp.bfloat16
    )
    outgoing = jnp.dot(picker, tile_rows, preferred_element_type=jnp.float32).astype(jnp.bfloat16)
    outgoing = outgoing.reshape(frame_total, low_pos, channels)
    gathered = lax.all_to_all(outgoing, "frame", split_axis=0, concat_axis=0, tiled=True)
    window_tiles = lax.dynamic_slice_in_dim(gathered, own_start, window_len, 0)
    cond = jnp.repeat(window_tiles, 4, axis=1)
    refined = refine(cond, noisy[0], cond_w, noise_w, gains, tconv, mlp_in, mlp_out)
    source_window = assign // TILES
    source_tile = assign % TILES
    placed = jnp.zeros((frame_total, tile_pos, channels), jnp.bfloat16)
    placed = lax.dynamic_update_slice_in_dim(placed, refined, own_start, 0)
    received = lax.all_to_all(placed, "frame", split_axis=0, concat_axis=0, tiled=True)
    offset = own_index - starts[source_window]
    inside = (offset >= 0) & (offset < window_len)
    clipped = jnp.clip(offset, 0, window_len - 1)
    factor = jnp.where(inside, blend[source_window, clipped], 0).astype(jnp.float32)
    tile_match = (source_tile[None, :] == jnp.arange(TILES, dtype=jnp.int32)[:, None]).astype(
        jnp.float32
    )
    blend_matrix = tile_match * factor[None, :]
    weighted = jnp.dot(
        blend_matrix.astype(jnp.bfloat16),
        received.reshape(frame_total, tile_pos * channels),
        preferred_element_type=jnp.float32,
    )
    denom = jnp.sum(blend_matrix, axis=1)
    video = weighted / denom[:, None]
    return video.reshape(1, TILES * tile_pos, channels).astype(jnp.bfloat16)


def solution(mesh):
    in_specs = (
        P(("groups", "frame"), None, None),
        P(("groups", "frame"), None, None, None),
        P("groups"),
        P("groups", None),
        P("groups"),
        P(),
        P(),
        P(),
        P(),
        P(),
        P(),
        P(),
    )
    out_specs = P(("groups", "frame"), None, None)
    return jax.shard_map(
        on_device, mesh=mesh, in_specs=in_specs, out_specs=out_specs, check_vma=False
    )
```

profile of v0, /device:TPU:0, one launch (start us, length us, event | category | flops | bytes accessed | tf_op | source)
XLA Modules:
  0.0 52.0 jit_solution(3728004417824354756)
XLA Ops:
  0.0 1.4 %collective-permute-start.1 = (bf16[1,64,128]{2,1,0:T(8,128)(2,1)}, bf16[1,64,128]{2,1,0:T(8,128)(2,1)S(1)}, u32[]{:S(2)}, u32[]{:S(2)}) collective-permute-start(bf16[1,64,128]{2,1,0:T(8,128)(2,1)} %param.12), channel_id=1, source_target_pairs={{1,0},{2,1},{3,2},{4,3},{5,4},{6,5},{7,6},{8,7},{9,8},{10,9},{11,1... | collective-permute-start | bytes 49160 | tf_op jit(solution)/shard_map/ppermute | solution.py:19
  1.4 3.0 %collective-permute-start = (bf16[1,64,128]{2,1,0:T(8,128)(2,1)}, bf16[1,64,128]{2,1,0:T(8,128)(2,1)S(1)}, u32[]{:S(2)}, u32[]{:S(2)}) collective-permute-start(bf16[1,64,128]{2,1,0:T(8,128)(2,1)} %param.12), channel_id=1, source_target_pairs={{0,1},{1,2},{2,3},{3,4},{4,5},{5,6},{6,7},{7,8},{8,9},{9,10},{10,1... | collective-permute-start | bytes 49160 | tf_op jit(solution)/shard_map/ppermute | solution.py:17
  4.5 0.7 %compare_select_fusion.1 = (s32[16]{0:T(128)S(1)}, s32[16]{0:T(128)S(1)}) fusion(s32[16]{0:T(128)} %param.16), kind=kLoop, calls=%fused_computation.58 | loop fusion | flops 352 | bytes 192 | tf_op jit(solution)/shard_map/select_n | solution.py:101
  5.1 0.9 %fusion.29 = f32[64,128]{1,0:T(8,128)S(1)} fusion(bf16[3,128,128]{2,1,0:T(8,128)(2,1)} %param.17, bf16[1,64,128]{2,1,0:T(8,128)(2,1)} %param.12), kind=kOutput, calls=%fused_computation.44 | convolution fusion | flops 2097152 | bytes 81920 | tf_op jit(solution)/shard_map/dot_general | solution.py:80
  6.1 0.6 %copy-done.11 = s32[16]{0:T(128)S(1)} copy-done((s32[16]{0:T(128)S(1)}, s32[16]{0:T(128)}, u32[]{:S(2)}) %copy-start.11) | copy-done | bytes 88
  6.7 0.6 %dynamic_slice.14 = s32[1]{0:T(128)} dynamic-slice(s32[16]{0:T(128)S(1)} %copy-done.11, s32[]{:T(128)S(6)} %select_n.58), dynamic_slice_sizes={1} | dynamic-slice | bytes 12 | tf_op jit(solution)/shard_map/dynamic_slice | solution.py:84
  9.9 0.6 %copy-done.1 = s32[4]{0:T(128)S(1)} copy-done((s32[4]{0:T(128)S(1)}, s32[4]{0:T(128)}, u32[]{:S(2)}) %copy-start.1) | copy-done | bytes 40
  10.6 0.6 %dynamic_slice.15 = s32[1]{0:T(128)} dynamic-slice(s32[4]{0:T(128)S(1)} %copy-done.1, s32[]{:T(128)S(6)} %select_n.60), dynamic_slice_sizes={1} | dynamic-slice | bytes 12 | tf_op jit(solution)/shard_map/dynamic_slice | solution.py:85
  12.5 0.7 %gather_fusion = s32[16]{0:T(128)S(1)} fusion(s32[4]{0:T(128)S(1)} %copy-done.1, s32[1024]{0:T(1024)S(1)} %pad_clamp_fusion), kind=kCustom, calls=%fused_computation | custom fusion | bytes 192 | tf_op jit(solution)/shard_map/gather | solution.py:101
  14.9 0.6 %copy.13 = bf16[2,8,16,128]{3,2,1,0:T(8,128)(2,1)} copy(bf16[2,8,16,128]{3,1,2,0:T(8,128)(2,1)S(1)} %fusion.2) | data formatting | bytes 131072
  15.6 8.1 %all-to-all-start = ((bf16[16,16,128]{2,1,0:T(8,128)(2,1)}), bf16[16,16,128]{2,1,0:T(8,128)(2,1)S(1)}, u32[]{:S(2)}, u32[]{:S(2)}) async-start(bf16[16,16,128]{2,1,0:T(8,128)(2,1)} %bitcast.45), calls=%async_computation | async-start | bytes 131072 | tf_op jit(solution)/shard_map/all_to_all | solution.py:92
  23.7 6.9 %all-to-all-done = bf16[16,16,128]{2,1,0:T(8,128)(2,1)S(1)} async-done(((bf16[16,16,128]{2,1,0:T(8,128)(2,1)}), bf16[16,16,128]{2,1,0:T(8,128)(2,1)S(1)}, u32[]{:S(2)}, u32[]{:S(2)}) %all-to-all-start) | async-done | bytes 65568 | tf_op jit(solution)/shard_map/all_to_all | solution.py:92
  30.6 0.7 %copy-done.4 = bf16[128,128]{1,0:T(8,128)(2,1)S(1)} copy-done((bf16[128,128]{1,0:T(8,128)(2,1)S(1)}, bf16[128,128]{1,0:T(8,128)(2,1)}, u32[]{:S(2)}) %copy-start.4) | copy-done | bytes 32792
  31.5 0.6 %copy-done.5 = bf16[128,128]{1,0:T(8,128)(2,1)S(1)} copy-done((bf16[128,128]{1,0:T(8,128)(2,1)S(1)}, bf16[128,128]{1,0:T(8,128)(2,1)}, u32[]{:S(2)}) %copy-start.5) | copy-done | bytes 32792
  32.7 0.9 %copy-done.9 = bf16[3,512,128]{2,1,0:T(8,128)(2,1)S(1)} copy-done((bf16[3,512,128]{2,1,0:T(8,128)(2,1)S(1)}, bf16[3,512,128]{2,1,0:T(8,128)(2,1)}, u32[]{:S(2)}) %copy-start.9) | copy-done | bytes 393240
  33.7 0.6 %multiply_reduce_fusion.1 = (f32[512]{0:T(512)S(1)}, f32[512,128]{1,0:T(8,128)S(1)}) fusion(f32[512,128]{1,0:T(8,128)S(1)} %get-tuple-element.56, bf16[3,512,128]{2,1,0:T(8,128)(2,1)S(1)} %copy-done.9, bf16[512,128]{1,0:T(8,128)(2,1)S(1)} %bitcast.129, bf16[3,128,512]{2,1,0:T(8,128)(2,1)S(1)} %copy-done.10), kind=kOutput, calls=%fused_computation.26 | convolution fusion | flops 135724544 | bytes 919552 | tf_op jit(solution)/shard_map/while/body/eval_jaxpr/dot_general | solution.py:49
  34.6 0.6 %multiply_reduce_fusion = (f32[512]{0:T(512)S(1)}, f32[512,128]{1,0:T(8,128)S(1)}) fusion(f32[512,128]{1,0:T(8,128)S(1)} %get-tuple-element.58, bf16[3,512,128]{2,1,0:T(8,128)(2,1)S(1)} %copy-done.9, bf16[512,128]{1,0:T(8,128)(2,1)S(1)} %bitcast.130, bf16[3,128,512]{2,1,0:T(8,128)(2,1)S(1)} %copy-done.10), kind=kOutput, calls=%fused_computation.23 | convolution fusion | flops 135724544 | bytes 919552 | tf_op jit(solution)/shard_map/while/body/eval_jaxpr/dot_general | solution.py:49
  36.1 0.8 %broadcast_in_dim.18 = bf16[16,64,128]{2,1,0:T(8,128)(2,1)} broadcast(bf16[]{:T(256)} %constant.86.clone.1), dimensions={} | broadcast | bytes 262146 | tf_op jit(solution)/shard_map/broadcast_in_dim | solution.py:98
  36.9 0.7 %constant_dynamic-update-slice_fusion = bf16[16,64,128]{2,1,0:T(8,128)(2,1)} fusion(bf16[16,64,128]{2,1,0:T(8,128)(2,1)} %broadcast_in_dim.18, bf16[8,64,128]{2,1,0:T(8,128)(2,1)S(1)} %bitcast.128, s32[]{:T(128)S(6)} %select_n.61), kind=kLoop, calls=%fused_computation.89 | loop fusion | bytes 262148 | tf_op jit(solution)/shard_map/dynamic_update_slice | solution.py:99
  37.5 3.5 %all-to-all-start.1 = ((bf16[16,64,128]{2,1,0:T(8,128)(2,1)}), bf16[16,64,128]{2,1,0:T(8,128)(2,1)S(1)}, u32[]{:S(2)}, u32[]{:S(2)}) async-start(bf16[16,64,128]{2,1,0:T(8,128)(2,1)} %constant_dynamic-update-slice_fusion), calls=%async_computation.1 | async-start | bytes 524288 | tf_op jit(solution)/shard_map/all_to_all | solution.py:100
  41.1 0.7 %copy-done.2 = s32[4,8]{1,0:T(4,128)S(1)} copy-done((s32[4,8]{1,0:T(4,128)S(1)}, s32[4,8]{1,0:T(4,128)}, u32[]{:S(2)}) %copy-start.2) | copy-done | bytes 152
  41.7 0.7 %gather_fusion.1 = s32[16]{0:T(128)S(1)} fusion(s32[4,8]{1,0:T(4,128)S(1)} %copy-done.2, s32[16]{0:T(128)S(1)} %fusion.47), kind=kCustom, calls=%fused_computation.1 | custom fusion | bytes 256 | tf_op jit(solution)/shard_map/gather | solution.py:104
  42.6 8.5 %all-to-all-done.1 = bf16[16,64,128]{2,1,0:T(8,128)(2,1)S(1)} async-done(((bf16[16,64,128]{2,1,0:T(8,128)(2,1)}), bf16[16,64,128]{2,1,0:T(8,128)(2,1)S(1)}, u32[]{:S(2)}, u32[]{:S(2)}) %all-to-all-start.1) | async-done | bytes 262176 | tf_op jit(solution)/shard_map/all_to_all | solution.py:100
  51.3 0.7 %convert_element_type.88 = bf16[1,256,128]{2,1,0:T(8,128)(2,1)} reshape(bf16[4,8192]{1,0:T(4,128)(2,1)S(1)} %fusion) | data formatting | bytes 131072 | tf_op jit(solution)/shard_map/convert_element_type | solution.py:116
  (48 shorter events, 3.4 us)
Async XLA Ops:
  0.0 31.5 %copy-start = (bf16[1,8,64,128]{3,2,1,0:T(8,128)(2,1)S(1)}, bf16[1,8,64,128]{3,2,1,0:T(8,128)(2,1)}, u32[]{:S(2)}) copy-start(bf16[1,8,64,128]{3,2,1,0:T(8,128)(2,1)} %param.13) | copy-start | bytes 393220
  0.0 13.8 %collective-permute-start.1 = (bf16[1,64,128]{2,1,0:T(8,128)(2,1)}, bf16[1,64,128]{2,1,0:T(8,128)(2,1)S(1)}, u32[]{:S(2)}, u32[]{:S(2)}) collective-permute-start(bf16[1,64,128]{2,1,0:T(8,128)(2,1)} %param.12), channel_id=1, source_target_pairs={{1,0},{2,1},{3,2},{4,3},{5,4},{6,5},{7,6},{8,7},{9,8},{10,9},{11,1... | collective-permute-start | bytes 49160 | tf_op jit(solution)/shard_map/ppermute | solution.py:19
  1.4 12.5 %collective-permute-start = (bf16[1,64,128]{2,1,0:T(8,128)(2,1)}, bf16[1,64,128]{2,1,0:T(8,128)(2,1)S(1)}, u32[]{:S(2)}, u32[]{:S(2)}) collective-permute-start(bf16[1,64,128]{2,1,0:T(8,128)(2,1)} %param.12), channel_id=1, source_target_pairs={{0,1},{1,2},{2,3},{3,4},{4,5},{5,6},{6,7},{7,8},{8,9},{9,10},{10,1... | collective-permute-start | bytes 49160 | tf_op jit(solution)/shard_map/ppermute | solution.py:17
  5.1 0.9 %copy-start.7 = (f32[3,3,128]{2,1,0:T(4,128)S(1)}, f32[3,3,128]{2,1,0:T(4,128)}, u32[]{:S(2)}) copy-start(f32[3,3,128]{2,1,0:T(4,128)} %param.21) | copy-start | bytes 13828
  6.1 0.7 %copy-start.11 = (s32[16]{0:T(128)S(1)}, s32[16]{0:T(128)}, u32[]{:S(2)}) copy-start(s32[16]{0:T(128)} %param.16) | copy-start | bytes 196
  9.9 0.7 %copy-start.1 = (s32[4]{0:T(128)S(1)}, s32[4]{0:T(128)}, u32[]{:S(2)}) copy-start(s32[4]{0:T(128)} %param.14) | copy-start | bytes 52
  12.5 1.4 %copy-start.3 = (bf16[3,128,128]{2,1,0:T(8,128)(2,1)S(1)}, bf16[3,128,128]{2,1,0:T(8,128)(2,1)}, u32[]{:S(2)}) copy-start(bf16[3,128,128]{2,1,0:T(8,128)(2,1)} %param.17) | copy-start | bytes 294916
  13.8 0.7 %copy-start.6 = (bf16[1,64,128]{2,1,0:T(8,128)(2,1)S(1)}, bf16[1,64,128]{2,1,0:T(8,128)(2,1)}, u32[]{:S(2)}) copy-start(bf16[1,64,128]{2,1,0:T(8,128)(2,1)} %param.12) | copy-start | bytes 49156
  15.6 8.1 %copy-start.8 = (f32[3,128]{1,0:T(4,128)S(1)}, f32[3,128]{1,0:T(4,128)}, u32[]{:S(2)}) copy-start(f32[3,128]{1,0:T(4,128)} %param.20) | copy-start | bytes 4612
  15.6 15.0 %all-to-all-start = ((bf16[16,16,128]{2,1,0:T(8,128)(2,1)}), bf16[16,16,128]{2,1,0:T(8,128)(2,1)S(1)}, u32[]{:S(2)}, u32[]{:S(2)}) async-start(bf16[16,16,128]{2,1,0:T(8,128)(2,1)} %bitcast.45), calls=%async_computation | async-start | bytes 131072 | tf_op jit(solution)/shard_map/all_to_all | solution.py:92
  30.6 0.8 %copy-start.4 = (bf16[128,128]{1,0:T(8,128)(2,1)S(1)}, bf16[128,128]{1,0:T(8,128)(2,1)}, u32[]{:S(2)}) copy-start(bf16[128,128]{1,0:T(8,128)(2,1)} %param.18) | copy-start | bytes 98308
  31.3 0.8 %copy-start.5 = (bf16[128,128]{1,0:T(8,128)(2,1)S(1)}, bf16[128,128]{1,0:T(8,128)(2,1)}, u32[]{:S(2)}) copy-start(bf16[128,128]{1,0:T(8,128)(2,1)} %param.19) | copy-start | bytes 98308
  32.6 1.0 %copy-start.9 = (bf16[3,512,128]{2,1,0:T(8,128)(2,1)S(1)}, bf16[3,512,128]{2,1,0:T(8,128)(2,1)}, u32[]{:S(2)}) copy-start(bf16[3,512,128]{2,1,0:T(8,128)(2,1)} %param.23) | copy-start | bytes 1179652
  32.6 1.1 %copy-start.10 = (bf16[3,128,512]{2,1,0:T(8,128)(2,1)S(1)}, bf16[3,128,512]{2,1,0:T(8,128)(2,1)}, u32[]{:S(2)}) copy-start(bf16[3,128,512]{2,1,0:T(8,128)(2,1)} %param.22) | copy-start | bytes 1179652
  37.5 13.5 %all-to-all-start.1 = ((bf16[16,64,128]{2,1,0:T(8,128)(2,1)}), bf16[16,64,128]{2,1,0:T(8,128)(2,1)S(1)}, u32[]{:S(2)}, u32[]{:S(2)}) async-start(bf16[16,64,128]{2,1,0:T(8,128)(2,1)} %constant_dynamic-update-slice_fusion), calls=%async_computation.1 | async-start | bytes 524288 | tf_op jit(solution)/shard_map/all_to_all | solution.py:100
  41.1 0.7 %copy-start.2 = (s32[4,8]{1,0:T(4,128)S(1)}, s32[4,8]{1,0:T(4,128)}, u32[]{:S(2)}) copy-start(s32[4,8]{1,0:T(4,128)} %param.15) | copy-start | bytes 388
where the time goes:
time: 52.8 us; the launch traced here: 52 us
  starting transfers between devices  16.1 us (30%)
  waiting for transfers between devices  15.4 us (29%)
  local copies, waits for them, and re-layouts  10.3 us (20%)
  between operations  4.86 us (9%)
  matrix products  3.93 us (7%)
  other arithmetic  1.47 us (3%)
    all_to_all x1, waiting for transfers between devices, on_device(): lax.all_to_all(placed, 'frame', split_axis=0, concat_axis=0, tiled=True)  8.48 us
    all_to_all x1, starting transfers between devices, on_device(): lax.all_to_all(outgoing, 'frame', split_axis=0, concat_axis=0, tiled=True)  8.11 us
    all_to_all x1, waiting for transfers between devices, on_device(): lax.all_to_all(outgoing, 'frame', split_axis=0, concat_axis=0, tiled=True)  6.87 us
    unnamed x25, local copies, waits for them, and re-layouts  5.51 us
    all_to_all x1, starting transfers between devices, on_device(): lax.all_to_all(placed, 'frame', split_axis=0, concat_axis=0, tiled=True)  3.53 us
    ppermute x1, starting transfers between devices, padded_2(): lax.ppermute(tail, axis, [(i, (i + 1) % count) for i in range(ends)])  3.04 us
    dot_general x3, matrix products, refine_block(): jnp.dot(hidden, mlp_out[layer_id], preferred_element_type=jnp.float32)  1.83 us
    ppermute x1, starting transfers between devices, padded_2(): lax.ppermute(head, axis, [((i + 1) % count, i) for i in range(ends)])  1.41 us
  transfers between devices with their start and end apart: 4, of which 2 were waited for; matrix products, arithmetic and copies ran while one was open for 8% of the time, Pallas kernels for 0%

commit v1 on v0

--- a/solution.py
+++ b/solution.py
@@ -4,6 +4,17 @@
 from jax.sharding import PartitionSpec as P
 
 TILES = 4
+
+
+def in_blocks(x, dim, peers):
+    before, after = (x.shape[:dim], x.shape[dim + 1 :])
+    return jnp.moveaxis(x.reshape(*before, peers, -1, *after), dim, 0)
+
+
+def laid_out(parts, dim):
+    shape = list(parts.shape[1:])
+    shape[dim] *= parts.shape[0]
+    return jnp.moveaxis(parts, 0, dim).reshape(shape)
 
 
 def padded_2(cells, sides, width):
@@ -89,7 +100,14 @@
     )
     outgoing = jnp.dot(picker, tile_rows, preferred_element_type=jnp.float32).astype(jnp.bfloat16)
     outgoing = outgoing.reshape(frame_total, low_pos, channels)
-    gathered = lax.all_to_all(outgoing, "frame", split_axis=0, concat_axis=0, tiled=True)
+    length, position = (lax.axis_size("frame"), lax.axis_index("frame"))
+    parts = in_blocks(outgoing, 0, length)
+    done = [parts[position]]
+    for step in range(1, length):
+        sent = parts[position ^ step]
+        done.append(lax.ppermute(sent, "frame", [(i_2, i_2 ^ step) for i_2 in range(length)]))
+    parts = jnp.stack(done)[position ^ jnp.arange(length)]
+    gathered = laid_out(parts, 0)
     window_tiles = lax.dynamic_slice_in_dim(gathered, own_start, window_len, 0)
     cond = jnp.repeat(window_tiles, 4, axis=1)
     refined = refine(cond, noisy[0], cond_w, noise_w, gains, tconv, mlp_in, mlp_out)

time: 52.8 us -> 65.7 us (1.24)
  starting transfers between devices: 16.1 us -> 31.9 us
  waiting for transfers between devices: 15.4 us -> 12.9 us
    ppermute x0 -> x15, starting transfers between devices: none -> 23.9 us  [on_device(): lax.ppermute(sent, 'frame', [(i_2, i_2 ^ step) for i_2 in range(length)])]
    all_to_all x1 -> x0, starting transfers between devices: 8.11 us -> none  [on_device(): lax.all_to_all(outgoing, 'frame', split_axis=0, concat_axis=0, tiled=True)]
    all_to_all x1 -> x0, waiting for transfers between devices: 6.87 us -> none  [on_device(): lax.all_to_all(outgoing, 'frame', split_axis=0, concat_axis=0, tiled=True)]
    ppermute x0 -> x15, waiting for transfers between devices: none -> 4.44 us  [on_device(): lax.ppermute(sent, 'frame', [(i_2, i_2 ^ step) for i_2 in range(length)])]
    select_n x1, other arithmetic: 0.67 us -> 0.01 us  [on_device(): offset = own_index - starts[source_window]]
    unnamed x25 -> x40, local copies, waits for them, and re-layouts: 5.51 us -> 4.98 us
  transfers between devices with their start and end apart: 4 -> 18, of which waited for: 2 -> 4; matrix products, arithmetic and copies ran while one was open for 8% -> 6% of each run, Pallas kernels for 0% -> 0%
where the time goes in v1:
time: 65.7 us; the launch traced here: 65.1 us
  starting transfers between devices  31.9 us (49%)
  waiting for transfers between devices  12.9 us (20%)
  local copies, waits for them, and re-layouts  10.4 us (16%)
  between operations  5.05 us (8%)
  matrix products  3.97 us (6%)
  other arithmetic  0.83 us (1%)
    ppermute x15, starting transfers between devices, on_device(): lax.ppermute(sent, 'frame', [(i_2, i_2 ^ step) for i_2 in range(length)])  23.9 us
    all_to_all x1, waiting for transfers between devices, on_device(): lax.all_to_all(placed, 'frame', split_axis=0, concat_axis=0, tiled=True)  8.48 us
    unnamed x40, local copies, waits for them, and re-layouts  4.98 us
    ppermute x15, waiting for transfers between devices, on_device(): lax.ppermute(sent, 'frame', [(i_2, i_2 ^ step) for i_2 in range(length)])  4.44 us
    all_to_all x1, starting transfers between devices, on_device(): lax.all_to_all(placed, 'frame', split_axis=0, concat_axis=0, tiled=True)  3.53 us
    ppermute x1, starting transfers between devices, padded_2(): lax.ppermute(tail, axis, [(i, (i + 1) % count) for i in range(ends)])  3.04 us
    dot_general x3, matrix products, refine_block(): jnp.dot(hidden, mlp_out[layer_id], preferred_element_type=jnp.float32)  1.83 us
    ppermute x1, starting transfers between devices, padded_2(): lax.ppermute(head, axis, [((i + 1) % count, i) for i in range(ends)])  1.41 us
  transfers between devices with their start and end apart: 18, of which 4 were waited for; matrix products, arithmetic and copies ran while one was open for 6% of the time, Pallas kernels for 0%

profile of v1, /device:TPU:0, one launch (start us, length us, event | category | flops | bytes accessed | tf_op | source)
XLA Modules:
  0.0 65.1 jit_solution(11077521934064456043)
XLA Ops:
  0.0 1.4 %collective-permute-start.1 = (bf16[1,64,128]{2,1,0:T(8,128)(2,1)}, bf16[1,64,128]{2,1,0:T(8,128)(2,1)S(1)}, u32[]{:S(2)}, u32[]{:S(2)}) collective-permute-start(bf16[1,64,128]{2,1,0:T(8,128)(2,1)} %param.12), channel_id=1, source_target_pairs={{1,0},{2,1},{3,2},{4,3},{5,4},{6,5},{7,6},{8,7},{9,8},{10,9},{11,1... | collective-permute-start | bytes 49160 | tf_op jit(solution)/shard_map/ppermute | solution.py:30
  1.4 3.0 %collective-permute-start = (bf16[1,64,128]{2,1,0:T(8,128)(2,1)}, bf16[1,64,128]{2,1,0:T(8,128)(2,1)S(1)}, u32[]{:S(2)}, u32[]{:S(2)}) collective-permute-start(bf16[1,64,128]{2,1,0:T(8,128)(2,1)} %param.12), channel_id=1, source_target_pairs={{0,1},{1,2},{2,3},{3,4},{4,5},{5,6},{6,7},{7,8},{8,9},{9,10},{10,1... | collective-permute-start | bytes 49160 | tf_op jit(solution)/shard_map/ppermute | solution.py:28
  5.2 0.9 %fusion.29 = f32[64,128]{1,0:T(8,128)S(1)} fusion(bf16[3,128,128]{2,1,0:T(8,128)(2,1)} %param.17, bf16[1,64,128]{2,1,0:T(8,128)(2,1)} %param.12), kind=kOutput, calls=%fused_computation.61 | convolution fusion | flops 2097152 | bytes 81920 | tf_op jit(solution)/shard_map/dot_general | solution.py:91
  7.5 2.7 %collective-permute-start.2 = (bf16[1,16,128]{2,1,0:T(8,128)(2,1)S(1)}, bf16[1,16,128]{2,1,0:T(8,128)(2,1)S(1)}, u32[]{:S(2)}, u32[]{:S(2)}) collective-permute-start(bf16[1,16,128]{2,1,0:T(8,128)(2,1)S(1)} %get-tuple-element.55), channel_id=1, source_target_pairs={{0,1},{1,0},{2,3},{3,2},{4,5},{5,4},{6,7},{7,6},{8,9},{9,8},{10,11... | collective-permute-start | bytes 12296 | tf_op jit(solution)/shard_map/ppermute | solution.py:108
  15.9 0.7 %gather_fusion = s32[16]{0:T(128)S(1)} fusion(s32[4]{0:T(128)S(1)} %copy-done.1, s32[1024]{0:T(1024)S(1)} %pad_clamp_fusion.1), kind=kCustom, calls=%fused_computation | custom fusion | bytes 192 | tf_op jit(solution)/shard_map/gather | solution.py:119
  17.2 2.4 %collective-permute-start.3 = (bf16[1,16,128]{2,1,0:T(8,128)(2,1)S(1)}, bf16[1,16,128]{2,1,0:T(8,128)(2,1)S(1)}, u32[]{:S(2)}, u32[]{:S(2)}) collective-permute-start(bf16[1,16,128]{2,1,0:T(8,128)(2,1)S(1)} %get-tuple-element.54), channel_id=1, source_target_pairs={{0,2},{1,3},{2,0},{3,1},{4,6},{5,7},{6,4},{7,5},{8,10},{9,11},{10,... | collective-permute-start | bytes 12296 | tf_op jit(solution)/shard_map/ppermute | solution.py:108
  19.6 2.0 %collective-permute-start.5 = (bf16[1,16,128]{2,1,0:T(8,128)(2,1)S(1)}, bf16[1,16,128]{2,1,0:T(8,128)(2,1)S(1)}, u32[]{:S(2)}, u32[]{:S(2)}) collective-permute-start(bf16[1,16,128]{2,1,0:T(8,128)(2,1)S(1)} %get-tuple-element.52), channel_id=1, source_target_pairs={{0,4},{1,5},{2,6},{3,7},{4,0},{5,1},{6,2},{7,3},{8,12},{9,13},{10,... | collective-permute-start | bytes 12296 | tf_op jit(solution)/shard_map/ppermute | solution.py:108
  21.7 2.5 %collective-permute-start.7 = (bf16[1,16,128]{2,1,0:T(8,128)(2,1)S(1)}, bf16[1,16,128]{2,1,0:T(8,128)(2,1)S(1)}, u32[]{:S(2)}, u32[]{:S(2)}) collective-permute-start(bf16[1,16,128]{2,1,0:T(8,128)(2,1)S(1)} %get-tuple-element.50), channel_id=1, source_target_pairs={{0,6},{1,7},{2,4},{3,5},{4,2},{5,3},{6,0},{7,1},{8,14},{9,15},{10,... | collective-permute-start | bytes 12296 | tf_op jit(solution)/shard_map/ppermute | solution.py:108
  24.2 2.9 %collective-permute-start.9 = (bf16[1,16,128]{2,1,0:T(8,128)(2,1)S(1)}, bf16[1,16,128]{2,1,0:T(8,128)(2,1)S(1)}, u32[]{:S(2)}, u32[]{:S(2)}) collective-permute-start(bf16[1,16,128]{2,1,0:T(8,128)(2,1)S(1)} %get-tuple-element.48), channel_id=1, source_target_pairs={{0,8},{1,9},{2,10},{3,11},{4,12},{5,13},{6,14},{7,15},{8,0},{9,1},... | collective-permute-start | bytes 12296 | tf_op jit(solution)/shard_map/ppermute | solution.py:108
  27.1 3.4 %collective-permute-start.11 = (bf16[1,16,128]{2,1,0:T(8,128)(2,1)S(1)}, bf16[1,16,128]{2,1,0:T(8,128)(2,1)S(1)}, u32[]{:S(2)}, u32[]{:S(2)}) collective-permute-start(bf16[1,16,128]{2,1,0:T(8,128)(2,1)S(1)} %get-tuple-element.46), channel_id=1, source_target_pairs={{0,10},{1,11},{2,8},{3,9},{4,14},{5,15},{6,12},{7,13},{8,2},{9,3},... | collective-permute-start | bytes 12296 | tf_op jit(solution)/shard_map/ppermute | solution.py:108
  30.5 3.8 %collective-permute-start.13 = (bf16[1,16,128]{2,1,0:T(8,128)(2,1)S(1)}, bf16[1,16,128]{2,1,0:T(8,128)(2,1)S(1)}, u32[]{:S(2)}, u32[]{:S(2)}) collective-permute-start(bf16[1,16,128]{2,1,0:T(8,128)(2,1)S(1)} %get-tuple-element.44), channel_id=1, source_target_pairs={{0,12},{1,13},{2,14},{3,15},{4,8},{5,9},{6,10},{7,11},{8,4},{9,5},... | collective-permute-start | bytes 12296 | tf_op jit(solution)/shard_map/ppermute | solution.py:108
  34.4 3.0 %collective-permute-start.15 = (bf16[1,16,128]{2,1,0:T(8,128)(2,1)S(1)}, bf16[1,16,128]{2,1,0:T(8,128)(2,1)S(1)}, u32[]{:S(2)}, u32[]{:S(2)}) collective-permute-start(bf16[1,16,128]{2,1,0:T(8,128)(2,1)S(1)} %get-tuple-element.40), channel_id=1, source_target_pairs={{0,14},{1,15},{2,12},{3,13},{4,10},{5,11},{6,8},{7,9},{8,6},{9,7},... | collective-permute-start | bytes 12296 | tf_op jit(solution)/shard_map/ppermute | solution.py:108
  37.4 1.3 %collective-permute-start.16 = (bf16[1,16,128]{2,1,0:T(8,128)(2,1)S(1)}, bf16[1,16,128]{2,1,0:T(8,128)(2,1)S(1)}, u32[]{:S(2)}, u32[]{:S(2)}) collective-permute-start(bf16[1,16,128]{2,1,0:T(8,128)(2,1)S(1)} %get-tuple-element.29), channel_id=1, source_target_pairs={{0,15},{1,14},{2,13},{3,12},{4,11},{5,10},{6,9},{7,8},{8,7},{9,6},... | collective-permute-start | bytes 12296 | tf_op jit(solution)/shard_map/ppermute | solution.py:108
  39.2 1.6 %collective-permute-done.15 = bf16[1,16,128]{2,1,0:T(8,128)(2,1)S(1)} collective-permute-done((bf16[1,16,128]{2,1,0:T(8,128)(2,1)S(1)}, bf16[1,16,128]{2,1,0:T(8,128)(2,1)S(1)}, u32[]{:S(2)}, u32[]{:S(2)}) %collective-permute-start.15) | collective-permute-done | bytes 4128 | tf_op jit(solution)/shard_map/ppermute | solution.py:108
  40.7 2.3 %collective-permute-done.16 = bf16[1,16,128]{2,1,0:T(8,128)(2,1)S(1)} collective-permute-done((bf16[1,16,128]{2,1,0:T(8,128)(2,1)S(1)}, bf16[1,16,128]{2,1,0:T(8,128)(2,1)S(1)}, u32[]{:S(2)}, u32[]{:S(2)}) %collective-permute-start.16) | collective-permute-done | bytes 4128 | tf_op jit(solution)/shard_map/ppermute | solution.py:108
  43.7 0.7 %copy-done.4 = bf16[128,128]{1,0:T(8,128)(2,1)S(1)} copy-done((bf16[128,128]{1,0:T(8,128)(2,1)S(1)}, bf16[128,128]{1,0:T(8,128)(2,1)}, u32[]{:S(2)}) %copy-start.4) | copy-done | bytes 32792
  45.8 0.9 %copy-done.9 = bf16[3,512,128]{2,1,0:T(8,128)(2,1)S(1)} copy-done((bf16[3,512,128]{2,1,0:T(8,128)(2,1)S(1)}, bf16[3,512,128]{2,1,0:T(8,128)(2,1)}, u32[]{:S(2)}) %copy-start.9) | copy-done | bytes 393240
  49.2 0.8 %broadcast_in_dim.17 = bf16[16,64,128]{2,1,0:T(8,128)(2,1)} broadcast(bf16[]{:T(256)} %constant.101.clone.1), dimensions={} | broadcast | bytes 262146 | tf_op jit(solution)/shard_map/broadcast_in_dim | solution.py:116
  50.0 0.6 constant_dynamic-update-slice_fusion.16
  50.6 3.5 %all-to-all-start = ((bf16[16,64,128]{2,1,0:T(8,128)(2,1)}), bf16[16,64,128]{2,1,0:T(8,128)(2,1)S(1)}, u32[]{:S(2)}, u32[]{:S(2)}) async-start(bf16[16,64,128]{2,1,0:T(8,128)(2,1)} %constant_dynamic-update-slice_fusion.16), calls=%async_computation | async-start | bytes 524288 | tf_op jit(solution)/shard_map/all_to_all | solution.py:118
  54.2 0.7 %copy-done.2 = s32[4,8]{1,0:T(4,128)S(1)} copy-done((s32[4,8]{1,0:T(4,128)S(1)}, s32[4,8]{1,0:T(4,128)}, u32[]{:S(2)}) %copy-start.2) | copy-done | bytes 152
  54.9 0.7 %gather_fusion.1 = s32[16]{0:T(128)S(1)} fusion(s32[4,8]{1,0:T(4,128)S(1)} %copy-done.2, s32[16]{0:T(128)S(1)} %fusion.63), kind=kCustom, calls=%fused_computation.1 | custom fusion | bytes 256 | tf_op jit(solution)/shard_map/gather | solution.py:122
  55.7 8.5 %all-to-all-done = bf16[16,64,128]{2,1,0:T(8,128)(2,1)S(1)} async-done(((bf16[16,64,128]{2,1,0:T(8,128)(2,1)}), bf16[16,64,128]{2,1,0:T(8,128)(2,1)S(1)}, u32[]{:S(2)}, u32[]{:S(2)}) %all-to-all-start) | async-done | bytes 262176 | tf_op jit(solution)/shard_map/all_to_all | solution.py:118
  64.4 0.7 %convert_element_type.88 = bf16[1,256,128]{2,1,0:T(8,128)(2,1)} reshape(bf16[4,8192]{1,0:T(4,128)(2,1)S(1)} %fusion) | data formatting | bytes 131072 | tf_op jit(solution)/shard_map/convert_element_type | solution.py:134
  (95 shorter events, 9.1 us)
Async XLA Ops:
  0.0 44.6 %copy-start = (bf16[1,8,64,128]{3,2,1,0:T(8,128)(2,1)S(1)}, bf16[1,8,64,128]{3,2,1,0:T(8,128)(2,1)}, u32[]{:S(2)}) copy-start(bf16[1,8,64,128]{3,2,1,0:T(8,128)(2,1)} %param.13) | copy-start | bytes 393220
  0.0 6.3 %collective-permute-start.1 = (bf16[1,64,128]{2,1,0:T(8,128)(2,1)}, bf16[1,64,128]{2,1,0:T(8,128)(2,1)S(1)}, u32[]{:S(2)}, u32[]{:S(2)}) collective-permute-start(bf16[1,64,128]{2,1,0:T(8,128)(2,1)} %param.12), channel_id=1, source_target_pairs={{1,0},{2,1},{3,2},{4,3},{5,4},{6,5},{7,6},{8,7},{9,8},{10,9},{11,1... | collective-permute-start | bytes 49160 | tf_op jit(solution)/shard_map/ppermute | solution.py:30
  1.4 5.0 %collective-permute-start = (bf16[1,64,128]{2,1,0:T(8,128)(2,1)}, bf16[1,64,128]{2,1,0:T(8,128)(2,1)S(1)}, u32[]{:S(2)}, u32[]{:S(2)}) collective-permute-start(bf16[1,64,128]{2,1,0:T(8,128)(2,1)} %param.12), channel_id=1, source_target_pairs={{0,1},{1,2},{2,3},{3,4},{4,5},{5,6},{6,7},{7,8},{8,9},{9,10},{10,1... | collective-permute-start | bytes 49160 | tf_op jit(solution)/shard_map/ppermute | solution.py:28
  5.1 1.0 %copy-start.8 = (f32[3,128]{1,0:T(4,128)S(1)}, f32[3,128]{1,0:T(4,128)}, u32[]{:S(2)}) copy-start(f32[3,128]{1,0:T(4,128)} %param.20) | copy-start | bytes 4612
  5.1 1.0 %copy-start.7 = (f32[3,3,128]{2,1,0:T(4,128)S(1)}, f32[3,3,128]{2,1,0:T(4,128)}, u32[]{:S(2)}) copy-start(f32[3,3,128]{2,1,0:T(4,128)} %param.21) | copy-start | bytes 13828
  5.1 1.1 %copy-start.3 = (bf16[3,128,128]{2,1,0:T(8,128)(2,1)S(1)}, bf16[3,128,128]{2,1,0:T(8,128)(2,1)}, u32[]{:S(2)}) copy-start(bf16[3,128,128]{2,1,0:T(8,128)(2,1)} %param.17) | copy-start | bytes 294916
  7.5 14.2 %collective-permute-start.2 = (bf16[1,16,128]{2,1,0:T(8,128)(2,1)S(1)}, bf16[1,16,128]{2,1,0:T(8,128)(2,1)S(1)}, u32[]{:S(2)}, u32[]{:S(2)}) collective-permute-start(bf16[1,16,128]{2,1,0:T(8,128)(2,1)S(1)} %get-tuple-element.55), channel_id=1, source_target_pairs={{0,1},{1,0},{2,3},{3,2},{4,5},{5,4},{6,7},{7,6},{8,9},{9,8},{10,11... | collective-permute-start | bytes 12296 | tf_op jit(solution)/shard_map/ppermute | solution.py:108
  17.2 6.9 %collective-permute-start.3 = (bf16[1,16,128]{2,1,0:T(8,128)(2,1)S(1)}, bf16[1,16,128]{2,1,0:T(8,128)(2,1)S(1)}, u32[]{:S(2)}, u32[]{:S(2)}) collective-permute-start(bf16[1,16,128]{2,1,0:T(8,128)(2,1)S(1)} %get-tuple-element.54), channel_id=1, source_target_pairs={{0,2},{1,3},{2,0},{3,1},{4,6},{5,7},{6,4},{7,5},{8,10},{9,11},{10,... | collective-permute-start | bytes 12296 | tf_op jit(solution)/shard_map/ppermute | solution.py:108
  19.6 4.5 %collective-permute-start.4 = (bf16[1,16,128]{2,1,0:T(8,128)(2,1)S(1)}, bf16[1,16,128]{2,1,0:T(8,128)(2,1)S(1)}, u32[]{:S(2)}, u32[]{:S(2)}) collective-permute-start(bf16[1,16,128]{2,1,0:T(8,128)(2,1)S(1)} %get-tuple-element.53), channel_id=1, source_target_pairs={{0,3},{1,2},{2,1},{3,0},{4,7},{5,6},{6,5},{7,4},{8,11},{9,10},{10,... | collective-permute-start | bytes 12296 | tf_op jit(solution)/shard_map/ppermute | solution.py:108
  19.6 7.5 %collective-permute-start.5 = (bf16[1,16,128]{2,1,0:T(8,128)(2,1)S(1)}, bf16[1,16,128]{2,1,0:T(8,128)(2,1)S(1)}, u32[]{:S(2)}, u32[]{:S(2)}) collective-permute-start(bf16[1,16,128]{2,1,0:T(8,128)(2,1)S(1)} %get-tuple-element.52), channel_id=1, source_target_pairs={{0,4},{1,5},{2,6},{3,7},{4,0},{5,1},{6,2},{7,3},{8,12},{9,13},{10,... | collective-permute-start | bytes 12296 | tf_op jit(solution)/shard_map/ppermute | solution.py:108
  21.7 5.5 %collective-permute-start.6 = (bf16[1,16,128]{2,1,0:T(8,128)(2,1)S(1)}, bf16[1,16,128]{2,1,0:T(8,128)(2,1)S(1)}, u32[]{:S(2)}, u32[]{:S(2)}) collective-permute-start(bf16[1,16,128]{2,1,0:T(8,128)(2,1)S(1)} %get-tuple-element.51), channel_id=1, source_target_pairs={{0,5},{1,4},{2,7},{3,6},{4,1},{5,0},{6,3},{7,2},{8,13},{9,12},{10,... | collective-permute-start | bytes 12296 | tf_op jit(solution)/shard_map/ppermute | solution.py:108
  21.7 8.8 %collective-permute-start.7 = (bf16[1,16,128]{2,1,0:T(8,128)(2,1)S(1)}, bf16[1,16,128]{2,1,0:T(8,128)(2,1)S(1)}, u32[]{:S(2)}, u32[]{:S(2)}) collective-permute-start(bf16[1,16,128]{2,1,0:T(8,128)(2,1)S(1)} %get-tuple-element.50), channel_id=1, source_target_pairs={{0,6},{1,7},{2,4},{3,5},{4,2},{5,3},{6,0},{7,1},{8,14},{9,15},{10,... | collective-permute-start | bytes 12296 | tf_op jit(solution)/shard_map/ppermute | solution.py:108
  24.1 6.4 %collective-permute-start.8 = (bf16[1,16,128]{2,1,0:T(8,128)(2,1)S(1)}, bf16[1,16,128]{2,1,0:T(8,128)(2,1)S(1)}, u32[]{:S(2)}, u32[]{:S(2)}) collective-permute-start(bf16[1,16,128]{2,1,0:T(8,128)(2,1)S(1)} %get-tuple-element.49), channel_id=1, source_target_pairs={{0,7},{1,6},{2,5},{3,4},{4,3},{5,2},{6,1},{7,0},{8,15},{9,14},{10,... | collective-permute-start | bytes 12296 | tf_op jit(solution)/shard_map/ppermute | solution.py:108
  24.2 10.2 %collective-permute-start.9 = (bf16[1,16,128]{2,1,0:T(8,128)(2,1)S(1)}, bf16[1,16,128]{2,1,0:T(8,128)(2,1)S(1)}, u32[]{:S(2)}, u32[]{:S(2)}) collective-permute-start(bf16[1,16,128]{2,1,0:T(8,128)(2,1)S(1)} %get-tuple-element.48), channel_id=1, source_target_pairs={{0,8},{1,9},{2,10},{3,11},{4,12},{5,13},{6,14},{7,15},{8,0},{9,1},... | collective-permute-start | bytes 12296 | tf_op jit(solution)/shard_map/ppermute | solution.py:108
  27.1 7.3 %collective-permute-start.10 = (bf16[1,16,128]{2,1,0:T(8,128)(2,1)S(1)}, bf16[1,16,128]{2,1,0:T(8,128)(2,1)S(1)}, u32[]{:S(2)}, u32[]{:S(2)}) collective-permute-start(bf16[1,16,128]{2,1,0:T(8,128)(2,1)S(1)} %get-tuple-element.47), channel_id=1, source_target_pairs={{0,9},{1,8},{2,11},{3,10},{4,13},{5,12},{6,15},{7,14},{8,1},{9,0},... | collective-permute-start | bytes 12296 | tf_op jit(solution)/shard_map/ppermute | solution.py:108
  27.1 10.2 %collective-permute-start.11 = (bf16[1,16,128]{2,1,0:T(8,128)(2,1)S(1)}, bf16[1,16,128]{2,1,0:T(8,128)(2,1)S(1)}, u32[]{:S(2)}, u32[]{:S(2)}) collective-permute-start(bf16[1,16,128]{2,1,0:T(8,128)(2,1)S(1)} %get-tuple-element.46), channel_id=1, source_target_pairs={{0,10},{1,11},{2,8},{3,9},{4,14},{5,15},{6,12},{7,13},{8,2},{9,3},... | collective-permute-start | bytes 12296 | tf_op jit(solution)/shard_map/ppermute | solution.py:108
  30.5 8.1 %collective-permute-start.12 = (bf16[1,16,128]{2,1,0:T(8,128)(2,1)S(1)}, bf16[1,16,128]{2,1,0:T(8,128)(2,1)S(1)}, u32[]{:S(2)}, u32[]{:S(2)}) collective-permute-start(bf16[1,16,128]{2,1,0:T(8,128)(2,1)S(1)} %get-tuple-element.45), channel_id=1, source_target_pairs={{0,11},{1,10},{2,9},{3,8},{4,15},{5,14},{6,13},{7,12},{8,3},{9,2},... | collective-permute-start | bytes 12296 | tf_op jit(solution)/shard_map/ppermute | solution.py:108
  30.5 8.1 %collective-permute-start.13 = (bf16[1,16,128]{2,1,0:T(8,128)(2,1)S(1)}, bf16[1,16,128]{2,1,0:T(8,128)(2,1)S(1)}, u32[]{:S(2)}, u32[]{:S(2)}) collective-permute-start(bf16[1,16,128]{2,1,0:T(8,128)(2,1)S(1)} %get-tuple-element.44), channel_id=1, source_target_pairs={{0,12},{1,13},{2,14},{3,15},{4,8},{5,9},{6,10},{7,11},{8,4},{9,5},... | collective-permute-start | bytes 12296 | tf_op jit(solution)/shard_map/ppermute | solution.py:108
  34.3 4.8 %collective-permute-start.14 = (bf16[1,16,128]{2,1,0:T(8,128)(2,1)S(1)}, bf16[1,16,128]{2,1,0:T(8,128)(2,1)S(1)}, u32[]{:S(2)}, u32[]{:S(2)}) collective-permute-start(bf16[1,16,128]{2,1,0:T(8,128)(2,1)S(1)} %get-tuple-element.42), channel_id=1, source_target_pairs={{0,13},{1,12},{2,15},{3,14},{4,9},{5,8},{6,11},{7,10},{8,5},{9,4},... | collective-permute-start | bytes 12296 | tf_op jit(solution)/shard_map/ppermute | solution.py:108
  34.4 6.4 %collective-permute-start.15 = (bf16[1,16,128]{2,1,0:T(8,128)(2,1)S(1)}, bf16[1,16,128]{2,1,0:T(8,128)(2,1)S(1)}, u32[]{:S(2)}, u32[]{:S(2)}) collective-permute-start(bf16[1,16,128]{2,1,0:T(8,128)(2,1)S(1)} %get-tuple-element.40), channel_id=1, source_target_pairs={{0,14},{1,15},{2,12},{3,13},{4,10},{5,11},{6,8},{7,9},{8,6},{9,7},... | collective-permute-start | bytes 12296 | tf_op jit(solution)/shard_map/ppermute | solution.py:108
  37.4 5.7 %collective-permute-start.16 = (bf16[1,16,128]{2,1,0:T(8,128)(2,1)S(1)}, bf16[1,16,128]{2,1,0:T(8,128)(2,1)S(1)}, u32[]{:S(2)}, u32[]{:S(2)}) collective-permute-start(bf16[1,16,128]{2,1,0:T(8,128)(2,1)S(1)} %get-tuple-element.29), channel_id=1, source_target_pairs={{0,15},{1,14},{2,13},{3,12},{4,11},{5,10},{6,9},{7,8},{8,7},{9,6},... | collective-permute-start | bytes 12296 | tf_op jit(solution)/shard_map/ppermute | solution.py:108
  45.7 1.0 %copy-start.9 = (bf16[3,512,128]{2,1,0:T(8,128)(2,1)S(1)}, bf16[3,512,128]{2,1,0:T(8,128)(2,1)}, u32[]{:S(2)}) copy-start(bf16[3,512,128]{2,1,0:T(8,128)(2,1)} %param.23) | copy-start | bytes 1179652
  45.7 1.1 %copy-start.10 = (bf16[3,128,512]{2,1,0:T(8,128)(2,1)S(1)}, bf16[3,128,512]{2,1,0:T(8,128)(2,1)}, u32[]{:S(2)}) copy-start(bf16[3,128,512]{2,1,0:T(8,128)(2,1)} %param.22) | copy-start | bytes 1179652
  50.6 13.5 %all-to-all-start = ((bf16[16,64,128]{2,1,0:T(8,128)(2,1)}), bf16[16,64,128]{2,1,0:T(8,128)(2,1)S(1)}, u32[]{:S(2)}, u32[]{:S(2)}) async-start(bf16[16,64,128]{2,1,0:T(8,128)(2,1)} %constant_dynamic-update-slice_fusion.16), calls=%async_computation | async-start | bytes 524288 | tf_op jit(solution)/shard_map/all_to_all | solution.py:118
  (6 other events, 4.2 us)
